TPU v7x, 256 devices: a whole 4x4x8 slice. The times are simulated.
256 devices in a mesh: ctx: 128 (over z, y_lo, x, core), dp: 2 (over y_hi).
Axes of the slice: x: 4, y: 4 (y_hi: 2, y_lo: 2; y = y_hi * 2 + y_lo), z: 8, core: 2. Of those that a mesh axis runs over, the one named last changes fastest.
Arguments:
- queries: bfloat16 [2, 2, 128, 64, 4096], P('dp', None, 'ctx'), may hold values from -6 to 6
- keys: bfloat16 [2, 2, 128, 64, 512], P('dp', None, 'ctx'), may hold values from -3 to 3
- values: bfloat16 [2, 2, 128, 64, 512], P('dp', None, 'ctx'), may hold values from -6 to 6
- cotangent: bfloat16 [2, 2, 128, 64, 4096], P('dp', None, 'ctx'), may hold values from -6 to 6
- doc_start: int32 [2, 2, 128, 64], P('dp', None, 'ctx'), may hold values from 0 to 16383, as said below
- loss_mask: int32 [2, 2, 128, 64], P('dp', None, 'ctx'), may hold values from 0 to 1, as said below
- seeds: int32 [2], P('dp'), may hold values from 0 to 999999
Outputs:
- attn_out: bfloat16 [2, 2, 128, 64, 4096], P('dp', None, 'ctx')
- grad_q: bfloat16 [2, 2, 128, 64, 4096], P('dp', None, 'ctx')
- grad_k: float32 [2, 2, 128, 64, 512], P('dp', None, 'ctx')
- grad_v: float32 [2, 2, 128, 64, 512], P('dp', None, 'ctx')
Inputs may be any that keep to these rules, and one draw needn't show every extreme that they name: `doc_start`: each entry is the position of the first token of its token's document; documents are runs of consecutive positions of at most 256 tokens, and the first document of each sequence has exactly that many. `loss_mask`: the token at position 0 of each sequence is counted.
All inputs are finite; a program needn't handle non-finite values.
Results may differ from a plain program's by a relative error of at most 0.038.
Values may be sent and summed in bfloat16 or wider, within the bound.
A program may use at most 64 MiB of HBM per device.

v0:
```python
import functools
import math

import jax
import jax.numpy as jnp
from jax import lax
from jax.experimental import pallas as pl
from jax.experimental.pallas import tpu as pltpu
from jax.sharding import PartitionSpec as P

SPAN = 64
GROUPS = 4
HEADS = 32
HEAD = 128
INV = 1.0 / math.sqrt(HEAD)
KEEP_SCALE = 1024.0 / 922.0
EXP2_SCALE = INV * math.log2(math.e)
MASKED = -1e30
MESH = pl.DeviceIdType.MESH


def nt(a, b):
    return lax.dot_general(a, b, (((1,), (1,)), ((), ())), preferred_element_type=jnp.float32)


def nn(a, b):
    return lax.dot_general(a, b, (((1,), (0,)), ((), ())), preferred_element_type=jnp.float32)


def keep_mask(mixed):
    mixed = mixed ^ lax.shift_right_arithmetic(mixed, 15)
    mixed = mixed * 73244475
    mixed = mixed ^ lax.shift_right_arithmetic(mixed, 13)
    mixed = mixed * 1274126177
    mixed = mixed ^ lax.shift_right_arithmetic(mixed, 16)
    return (mixed & 1023) >= 102


def relative_positions():
    row = lax.broadcasted_iota(jnp.int32, (256, 128), 0)
    offset = lax.broadcasted_iota(jnp.int32, (256, 128), 1) & 63
    tile = row >> 6
    inner = row & 63
    behind = jnp.where(tile == 3, jnp.where(inner <= offset, 0, 4), tile + 1)
    return inner - 64 * behind


def kernel(n, dims, q_hbm, do_hbm, k_hbm, v_hbm, start_ref, mask_ref, seed_ref,
           o_hbm, dq_hbm, dk_hbm, dv_hbm,
           q_ref, do_ref, o_ref, dq_ref, dqo_ref, dkv_ref,
           win, part, own, rx1, tot, rx2, rel_ref, mt_ref, pm_ref, ds_ref, acc, cbuf, fac_ref,
           in_sem, kv_sem, out_sem, kvout_sem,
           up_s, up_r, pt_s, pt_r, g1_s, g1_r, g2_s, g2_r, c_s, c_r):
    i = lax.axis_index("ctx")
    dp = lax.axis_index("dp")
    n_dp = lax.axis_size("dp")
    nz, ny, nx, nc = dims
    core = i % nc
    x = (i // nc) % nx
    ylo = (i // (nc * nx)) % ny
    z = i // (nc * nx * ny)
    partner = i + 1 - 2 * core
    spans = (i, 2 * n - 1 - i)
    rs = (core, 1 - core)

    def dev(c, d=dp):
        return {"ctx": c, "dp": d}

    def pdev(d):
        return jnp.where(i + d < n, i + d, 2 * n - 1 - i - d)

    def cidx(z_, y_, x_):
        return ((z_ * ny + y_) * nx + x_) * nc + core

    def count_peers(stage):
        peers = []
        if stage == 0:
            peers.append(dev(partner))
        elif stage == 1:
            for t in range(1, nx):
                peers.append(dev(cidx(z, ylo, (x + t) % nx)))
        elif stage == 2:
            both = dp * ny + ylo
            for t in range(1, ny * n_dp):
                other = (both + t) % (ny * n_dp)
                peers.append(dev(cidx(z, other % ny, x), other // ny))
        else:
            for t in range(1, nz):
                peers.append(dev(cidx((z + t) % nz, ylo, x)))
        return peers

    def count_copy(stage, t, target):
        return pltpu.make_async_remote_copy(
            acc.at[stage], cbuf.at[stage, t], c_s.at[stage, t], c_r.at[stage, t],
            device_id=target, device_id_type=MESH)

    def count_send(stage):
        for t, target in enumerate(count_peers(stage)):
            count_copy(stage, t, target).start()

    def count_take(stage):
        total = acc[stage]
        for t, target in enumerate(count_peers(stage)):
            cp = count_copy(stage, t, target)
            cp.wait_recv()
            cp.wait_send()
            total = total + cbuf[stage, t]
        acc[stage + 1] = total

    ins = []
    for h in range(2):
        for g in range(GROUPS):
            for w, src in enumerate((k_hbm, v_hbm)):
                cp = pltpu.make_async_copy(src.at[h, :, pl.ds(g * 128, 128)], win.at[g, h, 0, w], kv_sem.at[g, h, w])
                cp.start()
                ins.append(cp)
    cq = pltpu.make_async_copy(q_hbm, q_ref, in_sem.at[0])
    cd = pltpu.make_async_copy(do_hbm, do_ref, in_sem.at[1])
    cq.start()
    cd.start()

    barrier = pltpu.get_barrier_semaphore()

    def greet(target):
        pl.semaphore_signal(barrier, inc=1, device_id=target, device_id_type=MESH)

    n_greet = 0
    for d in (2, 4):
        greet(dev(pdev(d)))
        n_greet += 1
        pl.when(i >= d)(lambda d=d: greet(dev(i - d)))
    for stage in range(4):
        for target in count_peers(stage):
            greet(target)
            n_greet += 1

    rel_ref[...] = relative_positions()
    mask = mask_ref[...]
    acc[0] = jnp.pad(mask[0:1] + mask[1:2], ((0, 7), (0, 64)))
    for h in range(2):
        m = mask[h:h + 1].astype(jnp.float32)
        m2 = jnp.concatenate([m, m], axis=1)
        mt_ref[h] = jnp.broadcast_to(m2, (128, 128)).T.astype(jnp.bfloat16)
    for d in (2, 4):
        @pl.when(i < d)
        def _():
            win[:, 0, d] = jnp.zeros((GROUPS, 2, SPAN, HEAD), jnp.bfloat16)
            rx2[:, 1, d // 2 - 1] = jnp.zeros((GROUPS, 2, SPAN, HEAD), jnp.bfloat16)

    pl.semaphore_wait(barrier, n_greet + (i >= 2).astype(jnp.int32) + (i >= 4).astype(jnp.int32))

    def up_copy(g, h, d):
        e = d // 2 - 1
        if h == 0:
            half, target = jnp.where(i + d < n, 0, 1), dev(pdev(d))
        else:
            half, target = 1, dev(i - d)
        return pltpu.make_async_remote_copy(
            win.at[g, h, 0], win.at[g, half, d], up_s.at[g, h, e], up_r.at[g, half, e],
            device_id=target, device_id_type=MESH)

    def up_arrived(g, h, d):
        e = d // 2 - 1
        pltpu.make_async_remote_copy(
            win.at[g, h, d], win.at[g, h, d], up_s.at[g, h, e], up_r.at[g, h, e],
            device_id=dev(partner), device_id_type=MESH).wait_recv()

    def partner_copy(g, h, e):
        slot = 2 * rs[h] + 2 * e
        return pltpu.make_async_remote_copy(
            win.at[g, h, slot], win.at[g, h, 1 + 2 * e], pt_s.at[g, h, e], pt_r.at[g, h, e],
            device_id=dev(partner), device_id_type=MESH)

    for cp in ins:
        cp.wait()
    for g in range(GROUPS):
        for d in (4, 2):
            up_copy(g, 0, d).start()

            @pl.when(i >= d)
            def _():
                up_copy(g, 1, d).start()
    count_send(0)

    def relay(g):
        for d in (2, 4):
            pl.when(i >= d)(lambda d=d: up_arrived(g, 0, d))
            up_arrived(g, 1, d)
        for h in range(2):
            for e in range(2):
                partner_copy(g, h, e).start()

    count_take(0)
    count_send(1)
    cq.wait()
    cd.wait()
    relay(0)
    count_take(1)
    count_send(2)

    lane = lax.broadcasted_iota(jnp.int32, (1, 128), 1)
    tri = lax.broadcasted_iota(jnp.int32, (64, 128), 0) <= (lane & 63)

    def grad1_copy(g, h, e):
        return pltpu.make_async_remote_copy(
            part.at[g, h, 1 + 2 * e], rx1.at[g, h, e], g1_s.at[g, h, e], g1_r.at[g, h, e],
            device_id=dev(partner), device_id_type=MESH)

    def grad2_copy(g, h, d):
        e = d // 2 - 1
        if h == 0:
            half, target = 0, dev(i - d)
        else:
            half, target = jnp.where(i + d < n, 1, 0), dev(pdev(d))
        return pltpu.make_async_remote_copy(
            tot.at[g, h, e], rx2.at[g, half, e], g2_s.at[g, h, e], g2_r.at[g, half, e],
            device_id=target, device_id_type=MESH)

    def compute(g, h):
        span = spans[h]
        for e in range(2):
            partner_copy(g, h, e).wait_recv()
        kw = win[g, h, :, 0].reshape(320, 128)
        vw = win[g, h, :, 1].reshape(320, 128)
        kt = kw.T
        vt = vw.T
        start_row = start_ref[h:h + 1]
        start2 = jnp.concatenate([start_row, start_row], axis=1) - span * SPAN
        base = seed_ref[0] * 1000003 + span * SPAN * 9973
        mt = mt_ref[h, 0:64]
        col0 = (span * SPAN + (lane & 63)) * 40503 + base + (lane >> 6) * 7919

        def head_cols(j):
            return pl.ds(pl.multiple_of(g * 1024 + j * 128, 128), 128)

        for hh in range(2):
            q4 = jnp.concatenate([q_ref[h, :, head_cols(hh * 4 + j)] for j in range(4)], axis=0)
            d4 = jnp.concatenate([do_ref[h, :, head_cols(hh * 4 + j)] * mt for j in range(4)], axis=0)
            s4 = nt(kw, q4)
            g4 = nt(vw, d4)
            for pr in range(2):
                cs = slice(pr * 128, pr * 128 + 128)
                rel = rel_ref[...]
                keep = keep_mask(rel * 9973 + (col0 + (g * 8 + hh * 4 + pr * 2) * 7919))
                s = jnp.concatenate([s4[64:256, cs], jnp.where(tri, s4[:64, cs], s4[256:, cs])], axis=0)
                s = jnp.where(rel >= start2, s, MASKED)
                top = jnp.max(s, axis=0, keepdims=True)
                e = jnp.exp2((s - top) * EXP2_SCALE)
                p = e * (1.0 / jnp.sum(e, axis=0, keepdims=True))
                dp_ = jnp.concatenate([g4[64:256, cs], jnp.where(tri, g4[:64, cs], g4[256:, cs])], axis=0)
                gk = jnp.where(keep, dp_, 0.0)
                delta = jnp.sum(p * gk, axis=0, keepdims=True)
                ds = p * (gk - delta)
                pm = jnp.where(keep, p, 0.0)
                oc = slice(hh * 256 + pr * 128, hh * 256 + pr * 128 + 128)
                for ref, val in ((pm_ref, pm), (ds_ref, ds)):
                    ref[0:64, oc] = jnp.where(tri, val[192:], 0.0).astype(jnp.bfloat16)
                    ref[64:256, oc] = val[:192].astype(jnp.bfloat16)
                    ref[256:320, oc] = jnp.where(tri, 0.0, val[192:]).astype(jnp.bfloat16)
            ot = nn(vt, pm_ref[:, hh * 256:hh * 256 + 256]) * KEEP_SCALE
            dqt = nn(kt, ds_ref[:, hh * 256:hh * 256 + 256])
            oo = ot.T.astype(jnp.bfloat16)
            dq = dqt.T
            for j in range(4):
                o_ref[h, :, head_cols(hh * 4 + j)] = oo[j * 64:(j + 1) * 64]
                dq_ref[h, :, head_cols(hh * 4 + j)] = dq[j * 64:(j + 1) * 64]
        qall = jnp.concatenate([q_ref[h, :, head_cols(j)] for j in range(8)], axis=0)
        dall = jnp.concatenate([do_ref[h, :, head_cols(j)] * mt for j in range(8)], axis=0)
        dv = nn(pm_ref[...], dall)
        dk = nn(ds_ref[...], qall) * INV
        own[g, h, 0] = dk[0:64]
        own[g, h, 1] = dv[0:64]
        part[g, h, :, 0] = dk.reshape(5, SPAN, HEAD).astype(jnp.bfloat16)
        part[g, h, :, 1] = dv.reshape(5, SPAN, HEAD).astype(jnp.bfloat16)
        for e in range(2):
            grad1_copy(g, h, e).start()

    def combine(g, h):
        r = rs[h]
        rf = r.astype(jnp.float32)
        for e in range(2):
            grad1_copy(g, h, e).wait_recv()
        x1 = rx1[g, h, 0].astype(jnp.float32)
        x3 = rx1[g, h, 1].astype(jnp.float32)
        own[g, h] = own[g, h] + (1.0 - rf) * x1
        tot[g, h, 0] = (part[g, h, 2].astype(jnp.float32) + rf * x1 + (1.0 - rf) * x3).astype(jnp.bfloat16)
        tot[g, h, 1] = (part[g, h, 4].astype(jnp.float32) + rf * x3).astype(jnp.bfloat16)
        for d in (2, 4):
            if h == 0:
                pl.when(i >= d)(lambda d=d: grad2_copy(g, h, d).start())
            else:
                grad2_copy(g, h, d).start()

    def out_copy(which, g):
        src, dst = ((o_ref, o_hbm), (dqo_ref, dq_hbm))[which]
        cols = pl.ds(pl.multiple_of(g * 1024, 1024), 1024)
        return pltpu.make_async_copy(src.at[:, :, cols], dst.at[:, :, cols], out_sem.at[which, g])

    def finalize(g):
        cols = pl.ds(pl.multiple_of(g * 1024, 1024), 1024)
        scale = fac_ref[0:1, 0:1] * (KEEP_SCALE * INV)
        dqo_ref[:, :, cols] = (dq_ref[:, :, cols] * scale).astype(jnp.bfloat16)
        out_copy(1, g).start()

    count_take(2)
    count_send(3)

    def step(g, carry):
        compute(g, 0)

        @pl.when(g > 0)
        def _():
            combine(g - 1, 1)

        @pl.when(g < GROUPS - 1)
        def _():
            relay(g + 1)

        @pl.when(g == 1)
        def _():
            count_take(3)
            total = jnp.sum(acc[4].astype(jnp.float32))
            slots = float(2 * 2 * n * SPAN)
            fac_ref[...] = jnp.full((8, 128), slots, jnp.float32) / jnp.full((8, 128), total, jnp.float32)

        @pl.when(g > 0)
        def _():
            finalize(g - 1)

        compute(g, 1)
        combine(g, 0)
        out_copy(0, g).start()
        return carry

    lax.fori_loop(0, GROUPS, step, 0)
    combine(GROUPS - 1, 1)
    finalize(GROUPS - 1)

    def final(g, carry):
        for h in range(2):
            for d in (2, 4):
                def arrived(d=d):
                    e = d // 2 - 1
                    pltpu.make_async_remote_copy(
                        tot.at[g, h, e], rx2.at[g, h, e], g2_s.at[g, h, e], g2_r.at[g, h, e],
                        device_id=dev(partner), device_id_type=MESH).wait_recv()
                if h == 0:
                    arrived()
                else:
                    pl.when(i >= d)(arrived)
            scale = fac_ref[0:1, 0:1] * KEEP_SCALE
            val = (own[g, h] + rx2[g, h, 0].astype(jnp.float32) + rx2[g, h, 1].astype(jnp.float32)) * scale
            cols = pl.ds(pl.multiple_of(g * 128, 128), 128)
            dkv_ref[0, h, :, cols] = val[0]
            dkv_ref[1, h, :, cols] = val[1]
        return carry

    lax.fori_loop(0, GROUPS, final, 0)
    ck = pltpu.make_async_copy(dkv_ref.at[0], dk_hbm, kvout_sem.at[0])
    cv = pltpu.make_async_copy(dkv_ref.at[1], dv_hbm, kvout_sem.at[1])
    ck.start()
    cv.start()

    def drain(g, carry):
        for h in range(2):
            for e in range(2):
                d = 2 * e + 2
                partner_copy(g, h, e).wait_send()
                grad1_copy(g, h, e).wait_send()
                if h == 0:
                    up_copy(g, h, d).wait_send()
                    pl.when(i >= d)(lambda d=d: grad2_copy(g, 0, d).wait_send())
                else:
                    pl.when(i >= d)(lambda d=d: up_copy(g, 1, d).wait_send())
                    grad2_copy(g, h, d).wait_send()
        out_copy(0, g).wait()
        out_copy(1, g).wait()
        return carry

    lax.fori_loop(0, GROUPS, drain, 0)
    ck.wait()
    cv.wait()


def grid_of(n):
    nc, nx = 2, 4
    ny = 2 if n // (nc * nx) > 1 else 1
    return (n // (nc * nx * ny), ny, nx, nc)


def body(queries, keys, values, cotangent, doc_start, loss_mask, seeds):
    n = lax.axis_size("ctx")
    dims = grid_of(n)
    peers = max(1, dims[2] - 1, dims[1] * lax.axis_size("dp") - 1, dims[0] - 1)
    wide = (2, SPAN, HEADS * HEAD)
    narrow = (2, SPAN, GROUPS * HEAD)
    bf16, f32, i32 = jnp.bfloat16, jnp.float32, jnp.int32
    hbm = pl.BlockSpec(memory_space=pl.ANY)
    vmem = pl.BlockSpec(memory_space=pltpu.VMEM)
    dma = pltpu.SemaphoreType.DMA
    pair = (2, SPAN, HEAD)
    outs = pl.pallas_call(
        functools.partial(kernel, n, dims),
        out_shape=[
            jax.ShapeDtypeStruct(wide, bf16),
            jax.ShapeDtypeStruct(wide, bf16),
            jax.ShapeDtypeStruct(narrow, f32),
            jax.ShapeDtypeStruct(narrow, f32),
        ],
        in_specs=[hbm] * 4 + [vmem, vmem, pl.BlockSpec(memory_space=pltpu.SMEM)],
        out_specs=[hbm] * 4,
        scratch_shapes=[
            pltpu.VMEM(wide, bf16),
            pltpu.VMEM(wide, bf16),
            pltpu.VMEM(wide, bf16),
            pltpu.VMEM(wide, f32),
            pltpu.VMEM(wide, bf16),
            pltpu.VMEM((2,) + narrow, f32),
            pltpu.VMEM((GROUPS, 2, 5) + pair, bf16),
            pltpu.VMEM((GROUPS, 2, 5) + pair, bf16),
            pltpu.VMEM((GROUPS, 2) + pair, f32),
            pltpu.VMEM((GROUPS, 2, 2) + pair, bf16),
            pltpu.VMEM((GROUPS, 2, 2) + pair, bf16),
            pltpu.VMEM((GROUPS, 2, 2) + pair, bf16),
            pltpu.VMEM((256, 128), i32),
            pltpu.VMEM((2, 128, 128), bf16),
            pltpu.VMEM((320, 512), bf16),
            pltpu.VMEM((320, 512), bf16),
            pltpu.VMEM((5, 8, 128), i32),
            pltpu.VMEM((4, peers, 8, 128), i32),
            pltpu.VMEM((8, 128), f32),
            dma((2,)),
            dma((GROUPS, 2, 2)),
            dma((2, GROUPS)),
            dma((2,)),
        ] + [dma((GROUPS, 2, 2))] * 8 + [dma((4, peers))] * 2,
        compiler_params=pltpu.CompilerParams(collective_id=0, has_side_effects=True),
        name="attention",
    )(
        queries.reshape(wide),
        cotangent.reshape(wide),
        keys.reshape(narrow),
        values.reshape(narrow),
        doc_start.reshape(2, SPAN),
        loss_mask.reshape(2, SPAN),
        seeds,
    )
    return (
        outs[0].reshape(queries.shape),
        outs[1].reshape(queries.shape),
        outs[2].reshape(keys.shape),
        outs[3].reshape(values.shape),
    )


def solution(mesh):
    wide = P("dp", None, "ctx", None, None)
    flat = P("dp", None, "ctx", None)
    return jax.shard_map(
        body,
        mesh=mesh,
        in_specs=(wide, wide, wide, wide, flat, flat, P("dp")),
        out_specs=(wide, wide, wide, wide),
        check_vma=False,
    )
```

profile of v0, /device:TPU:9, one launch (start us, length us, event | category | flops | bytes accessed | tf_op | source)
XLA Modules:
  0.0 52.4 jit_solution(15282243242146235701)
XLA Ops:
  1.3 45.9 %attention.1 = (bf16[2,64,4096]{2,1,0:T(8,128)(2,1)}, bf16[2,64,4096]{2,1,0:T(8,128)(2,1)}, f32[2,64,512]{2,1,0:T(8,128)}, f32[2,64,512]{2,1,0:T(8,128)}) custom-call(bf16[2,64,4096]{2,1,0:T(8,128)(2,1)} %bitcast.18, bf16[2,64,4096]{2,1,0:T(8,128)(2,1)} %bitcast.19, bf16[2,64,512]{2,1,0:T(8,128)(2,1)} %bitcast.24, bf16[2,64,512]{2,1,0:T(8,128)(2,1)} %bitcast.25, ...), custom_call_target="tpu_custom_call" | custom-call | tf_op jit(solution)/shard_map/attention/pallas_call | solution.py:402
  47.2 0.0 copy-start
  47.2 2.4 %copy.20 = bf16[1,2,1,64,4096]{4,3,2,1,0:T(8,128)(2,1)} copy(bf16[1,2,1,64,4096]{4,3,2,1,0:T(8,128)(2,1)} %bitcast.21) | data formatting | bytes 2097152
  49.5 0.0 copy-done
  49.5 0.0 copy-start.2
  49.5 1.0 %copy.21 = bf16[1,2,1,64,4096]{4,3,2,1,0:T(8,128)(2,1)} copy(bf16[1,2,1,64,4096]{4,3,2,1,0:T(8,128)(2,1)S(1)} %bitcast.20) | data formatting | bytes 2097152
  50.5 0.1 copy-done.2
  50.6 0.0 copy-start.1
  50.6 0.7 %copy.22 = f32[1,2,1,64,512]{4,3,2,1,0:T(8,128)} copy(f32[1,2,1,64,512]{4,3,2,1,0:T(8,128)S(1)} %bitcast.23) | data formatting | bytes 524288
  51.3 0.3 copy-done.1
  51.7 0.7 %copy.23 = f32[1,2,1,64,512]{4,3,2,1,0:T(8,128)} copy(f32[1,2,1,64,512]{4,3,2,1,0:T(8,128)S(1)} %bitcast.22) | data formatting | bytes 524288
Async XLA Ops:
  47.2 2.4 %copy-start = (bf16[2,64,4096]{2,1,0:T(8,128)(2,1)S(1)}, bf16[2,64,4096]{2,1,0:T(8,128)(2,1)}, u32[]{:S(2)}) copy-start(bf16[2,64,4096]{2,1,0:T(8,128)(2,1)} %get-tuple-element.9) | copy-start | bytes 3145732
  49.5 1.1 %copy-start.2 = (f32[2,64,512]{2,1,0:T(8,128)S(1)}, f32[2,64,512]{2,1,0:T(8,128)}, u32[]{:S(2)}) copy-start(f32[2,64,512]{2,1,0:T(8,128)} %get-tuple-element.10) | copy-start | bytes 786436
  50.6 1.0 %copy-start.1 = (f32[2,64,512]{2,1,0:T(8,128)S(1)}, f32[2,64,512]{2,1,0:T(8,128)}, u32[]{:S(2)}) copy-start(f32[2,64,512]{2,1,0:T(8,128)} %get-tuple-element.11) | copy-start | bytes 786436
where the time goes:
time: 52.6 us; the launch traced here: 52.4 us
  Pallas kernels  45.9 us (87%)
  local copies, waits for them, and re-layouts  5.22 us (10%)
  between operations  1.3 us (2%)
    pallas_call x1, Pallas kernels, body(): pl.pallas_call(functools.partial(kernel, n, dims), out_shape=[jax.ShapeDt...  45.9 us
    unnamed x10, local copies, waits for them, and re-layouts  5.22 us

commit v1 on v0

--- a/solution.py
+++ b/solution.py
@@ -46,10 +46,10 @@
 
 
 def kernel(n, dims, q_hbm, do_hbm, k_hbm, v_hbm, start_ref, mask_ref, seed_ref,
-           o_hbm, dq_hbm, dk_hbm, dv_hbm,
-           q_ref, do_ref, o_ref, dq_ref, dqo_ref, dkv_ref,
-           win, part, own, rx1, tot, rx2, rel_ref, mt_ref, pm_ref, ds_ref, acc, cbuf, fac_ref,
-           in_sem, kv_sem, out_sem, kvout_sem,
+           o_ref, dqo_ref, dkv_ref,
+           q_ref, do_ref, dq_ref,
+           win, part, own, rx1, tot, rx2, keep_ref, bias_ref, mt_ref, pm_ref, ds_ref, acc, cbuf, fac_ref,
+           in_sem, kv_sem,
            up_s, up_r, pt_s, pt_r, g1_s, g1_r, g2_s, g2_r, c_s, c_r):
     i = lax.axis_index("ctx")
     dp = lax.axis_index("dp")
@@ -134,13 +134,16 @@
             greet(target)
             n_greet += 1
 
-    rel_ref[...] = relative_positions()
+    rel = relative_positions()
     mask = mask_ref[...]
     acc[0] = jnp.pad(mask[0:1] + mask[1:2], ((0, 7), (0, 64)))
     for h in range(2):
         m = mask[h:h + 1].astype(jnp.float32)
         m2 = jnp.concatenate([m, m], axis=1)
         mt_ref[h] = jnp.broadcast_to(m2, (128, 128)).T.astype(jnp.bfloat16)
+        start_row = start_ref[h:h + 1]
+        start2 = jnp.concatenate([start_row, start_row], axis=1) - spans[h] * SPAN
+        bias_ref[h] = jnp.where(rel >= start2, 0.0, MASKED)
     for d in (2, 4):
         @pl.when(i < d)
         def _():
@@ -190,16 +193,26 @@
             for e in range(2):
                 partner_copy(g, h, e).start()
 
-    count_take(0)
-    count_send(1)
+    lane = lax.broadcasted_iota(jnp.int32, (1, 128), 1)
+    tri = lax.broadcasted_iota(jnp.int32, (64, 128), 0) <= (lane & 63)
+
+    hashed = relative_positions() * 9973
+    for h in range(2):
+        base = seed_ref[0] * 1000003 + spans[h] * (SPAN * 9973)
+        col0 = (spans[h] * SPAN + (lane & 63)) * 40503 + base + (lane >> 6) * 7919
+
+        def fill(pair, carry, h=h, col0=col0):
+            keep = keep_mask(hashed + (col0 + pair * (2 * 7919)))
+            keep_ref[h, pair] = jnp.where(keep, 1.0, 0.0)
+            return carry
+
+        lax.fori_loop(0, HEADS // 2, fill, 0)
+
     cq.wait()
     cd.wait()
     relay(0)
-    count_take(1)
-    count_send(2)
-
-    lane = lax.broadcasted_iota(jnp.int32, (1, 128), 1)
-    tri = lax.broadcasted_iota(jnp.int32, (64, 128), 0) <= (lane & 63)
+    count_take(0)
+    count_send(1)
 
     def grad1_copy(g, h, e):
         return pltpu.make_async_remote_copy(
@@ -217,18 +230,13 @@
             device_id=target, device_id_type=MESH)
 
     def compute(g, h):
-        span = spans[h]
         for e in range(2):
             partner_copy(g, h, e).wait_recv()
         kw = win[g, h, :, 0].reshape(320, 128)
         vw = win[g, h, :, 1].reshape(320, 128)
         kt = kw.T
         vt = vw.T
-        start_row = start_ref[h:h + 1]
-        start2 = jnp.concatenate([start_row, start_row], axis=1) - span * SPAN
-        base = seed_ref[0] * 1000003 + span * SPAN * 9973
         mt = mt_ref[h, 0:64]
-        col0 = (span * SPAN + (lane & 63)) * 40503 + base + (lane >> 6) * 7919
 
         def head_cols(j):
             return pl.ds(pl.multiple_of(g * 1024 + j * 128, 128), 128)
@@ -240,18 +248,16 @@
             g4 = nt(vw, d4)
             for pr in range(2):
                 cs = slice(pr * 128, pr * 128 + 128)
-                rel = rel_ref[...]
-                keep = keep_mask(rel * 9973 + (col0 + (g * 8 + hh * 4 + pr * 2) * 7919))
                 s = jnp.concatenate([s4[64:256, cs], jnp.where(tri, s4[:64, cs], s4[256:, cs])], axis=0)
-                s = jnp.where(rel >= start2, s, MASKED)
+                s = s + bias_ref[h]
                 top = jnp.max(s, axis=0, keepdims=True)
                 e = jnp.exp2((s - top) * EXP2_SCALE)
                 p = e * (1.0 / jnp.sum(e, axis=0, keepdims=True))
+                pm = p * keep_ref[h, g * 4 + hh * 2 + pr]
                 dp_ = jnp.concatenate([g4[64:256, cs], jnp.where(tri, g4[:64, cs], g4[256:, cs])], axis=0)
-                gk = jnp.where(keep, dp_, 0.0)
-                delta = jnp.sum(p * gk, axis=0, keepdims=True)
-                ds = p * (gk - delta)
-                pm = jnp.where(keep, p, 0.0)
+                t = pm * dp_
+                delta = jnp.sum(t, axis=0, keepdims=True)
+                ds = t - p * delta
                 oc = slice(hh * 256 + pr * 128, hh * 256 + pr * 128 + 128)
                 for ref, val in ((pm_ref, pm), (ds_ref, ds)):
                     ref[0:64, oc] = jnp.where(tri, val[192:], 0.0).astype(jnp.bfloat16)
@@ -291,19 +297,10 @@
             else:
                 grad2_copy(g, h, d).start()
 
-    def out_copy(which, g):
-        src, dst = ((o_ref, o_hbm), (dqo_ref, dq_hbm))[which]
-        cols = pl.ds(pl.multiple_of(g * 1024, 1024), 1024)
-        return pltpu.make_async_copy(src.at[:, :, cols], dst.at[:, :, cols], out_sem.at[which, g])
-
     def finalize(g):
         cols = pl.ds(pl.multiple_of(g * 1024, 1024), 1024)
         scale = fac_ref[0:1, 0:1] * (KEEP_SCALE * INV)
         dqo_ref[:, :, cols] = (dq_ref[:, :, cols] * scale).astype(jnp.bfloat16)
-        out_copy(1, g).start()
-
-    count_take(2)
-    count_send(3)
 
     def step(g, carry):
         compute(g, 0)
@@ -316,25 +313,29 @@
         def _():
             relay(g + 1)
 
+        compute(g, 1)
+        combine(g, 0)
+
+        @pl.when(g == 0)
+        def _():
+            count_take(1)
+            count_send(2)
+
         @pl.when(g == 1)
         def _():
-            count_take(3)
-            total = jnp.sum(acc[4].astype(jnp.float32))
-            slots = float(2 * 2 * n * SPAN)
-            fac_ref[...] = jnp.full((8, 128), slots, jnp.float32) / jnp.full((8, 128), total, jnp.float32)
-
-        @pl.when(g > 0)
-        def _():
-            finalize(g - 1)
-
-        compute(g, 1)
-        combine(g, 0)
-        out_copy(0, g).start()
+            count_take(2)
+            count_send(3)
+
         return carry
 
     lax.fori_loop(0, GROUPS, step, 0)
     combine(GROUPS - 1, 1)
-    finalize(GROUPS - 1)
+    count_take(3)
+    total = jnp.sum(acc[4].astype(jnp.float32))
+    slots = float(2 * 2 * n * SPAN)
+    fac_ref[...] = jnp.full((8, 128), slots, jnp.float32) / jnp.full((8, 128), total, jnp.float32)
+    for g in range(GROUPS):
+        finalize(g)
 
     def final(g, carry):
         for h in range(2):
@@ -356,11 +357,6 @@
         return carry
 
     lax.fori_loop(0, GROUPS, final, 0)
-    ck = pltpu.make_async_copy(dkv_ref.at[0], dk_hbm, kvout_sem.at[0])
-    cv = pltpu.make_async_copy(dkv_ref.at[1], dv_hbm, kvout_sem.at[1])
-    ck.start()
-    cv.start()
-
     def drain(g, carry):
         for h in range(2):
             for e in range(2):
@@ -373,13 +369,22 @@
                 else:
                     pl.when(i >= d)(lambda d=d: up_copy(g, 1, d).wait_send())
                     grad2_copy(g, h, d).wait_send()
-        out_copy(0, g).wait()
-        out_copy(1, g).wait()
         return carry
 
     lax.fori_loop(0, GROUPS, drain, 0)
-    ck.wait()
-    cv.wait()
+
+
+def store_kernel(o_ref, dq_ref, dkv_ref, o_hbm, dq_hbm, dk_hbm, dv_hbm, sems):
+    copies = [
+        pltpu.make_async_copy(o_ref, o_hbm, sems.at[0]),
+        pltpu.make_async_copy(dq_ref, dq_hbm, sems.at[1]),
+        pltpu.make_async_copy(dkv_ref.at[0], dk_hbm, sems.at[2]),
+        pltpu.make_async_copy(dkv_ref.at[1], dv_hbm, sems.at[3]),
+    ]
+    for cp in copies:
+        cp.start()
+    for cp in copies:
+        cp.wait()
 
 
 def grid_of(n):
@@ -399,30 +404,23 @@
     vmem = pl.BlockSpec(memory_space=pltpu.VMEM)
     dma = pltpu.SemaphoreType.DMA
     pair = (2, SPAN, HEAD)
-    outs = pl.pallas_call(
+    held = pl.pallas_call(
         functools.partial(kernel, n, dims),
-        out_shape=[
-            jax.ShapeDtypeStruct(wide, bf16),
-            jax.ShapeDtypeStruct(wide, bf16),
-            jax.ShapeDtypeStruct(narrow, f32),
-            jax.ShapeDtypeStruct(narrow, f32),
-        ],
+        out_shape=[pltpu.VMEM(wide, bf16), pltpu.VMEM(wide, bf16), pltpu.VMEM((2,) + narrow, f32)],
         in_specs=[hbm] * 4 + [vmem, vmem, pl.BlockSpec(memory_space=pltpu.SMEM)],
-        out_specs=[hbm] * 4,
+        out_specs=[vmem] * 3,
         scratch_shapes=[
             pltpu.VMEM(wide, bf16),
             pltpu.VMEM(wide, bf16),
-            pltpu.VMEM(wide, bf16),
             pltpu.VMEM(wide, f32),
-            pltpu.VMEM(wide, bf16),
-            pltpu.VMEM((2,) + narrow, f32),
             pltpu.VMEM((GROUPS, 2, 5) + pair, bf16),
             pltpu.VMEM((GROUPS, 2, 5) + pair, bf16),
             pltpu.VMEM((GROUPS, 2) + pair, f32),
             pltpu.VMEM((GROUPS, 2, 2) + pair, bf16),
             pltpu.VMEM((GROUPS, 2, 2) + pair, bf16),
             pltpu.VMEM((GROUPS, 2, 2) + pair, bf16),
-            pltpu.VMEM((256, 128), i32),
+            pltpu.VMEM((2, HEADS // 2, 256, 128), f32),
+            pltpu.VMEM((2, 256, 128), f32),
             pltpu.VMEM((2, 128, 128), bf16),
             pltpu.VMEM((320, 512), bf16),
             pltpu.VMEM((320, 512), bf16),
@@ -431,8 +429,6 @@
             pltpu.VMEM((8, 128), f32),
             dma((2,)),
             dma((GROUPS, 2, 2)),
-            dma((2, GROUPS)),
-            dma((2,)),
         ] + [dma((GROUPS, 2, 2))] * 8 + [dma((4, peers))] * 2,
         compiler_params=pltpu.CompilerParams(collective_id=0, has_side_effects=True),
         name="attention",
@@ -445,6 +441,19 @@
         loss_mask.reshape(2, SPAN),
         seeds,
     )
+    outs = pl.pallas_call(
+        store_kernel,
+        out_shape=[
+            jax.ShapeDtypeStruct(wide, bf16),
+            jax.ShapeDtypeStruct(wide, bf16),
+            jax.ShapeDtypeStruct(narrow, f32),
+            jax.ShapeDtypeStruct(narrow, f32),
+        ],
+        in_specs=[vmem] * 3,
+        out_specs=[hbm] * 4,
+        scratch_shapes=[dma((4,))],
+        name="store",
+    )(*[pltpu.with_memory_space_constraint(x, pltpu.VMEM) for x in held])
     return (
         outs[0].reshape(queries.shape),
         outs[1].reshape(queries.shape),

time: 52.6 us -> 41.4 us (0.79)
  Pallas kernels: 45.9 us -> 40 us
  local copies, waits for them, and re-layouts: 5.22 us -> 0 us
    pallas_call x1 -> x2, Pallas kernels: 45.9 us -> 40 us  [the longest x1 38.5 us: body(): pl.pallas_call(functools.partial(kernel, n, dims), out_shape=[pltpu.VMEM(...]
    unnamed x10 -> x0, local copies, waits for them, and re-layouts: 5.22 us -> none
where the time goes in v1:
time: 41.4 us; the launch traced here: 41.3 us
  Pallas kernels  40 us (97%)
  between operations  1.29 us (3%)
    pallas_call x1, Pallas kernels, body(): pl.pallas_call(functools.partial(kernel, n, dims), out_shape=[pltpu.VMEM(...  38.5 us
    pallas_call x1, Pallas kernels, body(): pl.pallas_call(store_kernel, out_shape=[jax.ShapeDtypeStruct(wide, bf16),...  1.52 us

profile of v1, /device:TPU:9, one launch (start us, length us, event | category | flops | bytes accessed | tf_op | source)
XLA Modules:
  0.0 41.3 jit_solution(17936347894025341474)
XLA Ops:
  1.3 38.5 %attention.1 = (bf16[2,64,4096]{2,1,0:T(8,128)(2,1)S(1)}, bf16[2,64,4096]{2,1,0:T(8,128)(2,1)S(1)}, f32[2,2,64,512]{3,2,1,0:T(8,128)S(1)}) custom-call(bf16[2,64,4096]{2,1,0:T(8,128)(2,1)} %bitcast.18, bf16[2,64,4096]{2,1,0:T(8,128)(2,1)} %bitcast.19, bf16[2,64,512]{2,1,0:T(8,128)(2,1)} %bitcast.20, bf16[2,64,512]{2,1,0:T(8,128)(2,1)} %bitcast.21, ...), custom_call_target="tpu_custom_call" | custom-call | tf_op jit(solution)/shard_map/attention/pallas_call | solution.py:407
  39.8 1.5 %store.1 = (bf16[2,64,4096]{2,1,0:T(8,128)(2,1)}, bf16[2,64,4096]{2,1,0:T(8,128)(2,1)}, f32[2,64,512]{2,1,0:T(8,128)}, f32[2,64,512]{2,1,0:T(8,128)}) custom-call(bf16[2,64,4096]{2,1,0:T(8,128)(2,1)S(1)} %get-tuple-element.11.o_ref, bf16[2,64,4096]{2,1,0:T(8,128)(2,1)S(1)} %get-tuple-element.12.dq_ref, f32[2,2,64,512]{3,2,1,0:T(8,128)S(1)} %get-tuple-element.13.dkv_ref), custom_call_target="tpu_custom_call" | custom-call | tf_op jit(solution)/shard_map/store/pallas_call | solution.py:444

commit v2 on v1

v2 whole, which is shorter than its diff:
```python
import functools
import math

import jax
import jax.numpy as jnp
from jax import lax
from jax.experimental import pallas as pl
from jax.experimental.pallas import tpu as pltpu
from jax.sharding import PartitionSpec as P

SPAN = 64
GROUPS = 4
HEADS = 32
HEAD = 128
INV = 1.0 / math.sqrt(HEAD)
KEEP_SCALE = 1024.0 / 922.0
EXP2_SCALE = INV * math.log2(math.e)
MASKED = -1e30
MESH = pl.DeviceIdType.MESH


def nt(a, b):
    return lax.dot_general(a, b, (((1,), (1,)), ((), ())), preferred_element_type=jnp.float32)


def nn(a, b):
    return lax.dot_general(a, b, (((1,), (0,)), ((), ())), preferred_element_type=jnp.float32)


def keep_mask(mixed):
    mixed = mixed ^ lax.shift_right_arithmetic(mixed, 15)
    mixed = mixed * 73244475
    mixed = mixed ^ lax.shift_right_arithmetic(mixed, 13)
    mixed = mixed * 1274126177
    mixed = mixed ^ lax.shift_right_arithmetic(mixed, 16)
    return (mixed & 1023) >= 102


def relative_positions():
    row = lax.broadcasted_iota(jnp.int32, (256, 128), 0)
    offset = lax.broadcasted_iota(jnp.int32, (256, 128), 1) & 63
    tile = row >> 6
    inner = row & 63
    apart = jnp.where(tile == 0, 2, jnp.where(tile == 1, 1, 3))
    behind = jnp.where(tile == 3, jnp.where(inner <= offset, 0, 4), apart)
    return inner - 64 * behind


def kernel(n, dims, q_hbm, do_hbm, k_hbm, v_hbm, start_ref, mask_ref, seed_ref,
           o_ref, dqo_ref, dkv_ref,
           q_ref, do_ref,
           win, part, own, rx1, tot, rx2, keep_ref, bias_ref, mt_ref,
           s0_ref, s1_ref, d0_ref, d1_ref, pm00_ref, pm01_ref, pm10_ref, pm11_ref, ds00_ref, ds01_ref, ds10_ref, ds11_ref, sum_ref,
           acc, cbuf,
           in_sem, kv_sem,
           up_s, up_r, fw_s, fw_r, pt_s, pt_r, g1_s, g1_r, g2_s, g2_r, c_s, c_r):
    i = lax.axis_index("ctx")
    dp = lax.axis_index("dp")
    n_dp = lax.axis_size("dp")
    nz, ny, nx, nc = dims
    core = lax.rem(i, nc)
    x = lax.rem(lax.div(i, nc), nx)
    ylo = lax.rem(lax.div(i, nc * nx), ny)
    z = lax.div(i, nc * nx * ny)
    partner = i + 1 - 2 * core
    spans = (i, 2 * n - 1 - i)
    rs = (core, 1 - core)
    inside = i + 2 < n
    across = jnp.where(inside, i + 2, 2 * n - 3 - i)
    has_back = i >= 2
    inside4 = i + 4 < n
    across4 = jnp.where(inside4, i + 4, 2 * n - 5 - i)
    has_back4 = i >= 4

    def dev(c, d=dp):
        return {"ctx": c, "dp": d}

    def cidx(z_, y_, x_):
        return ((z_ * ny + y_) * nx + x_) * nc + core

    def count_peers(stage):
        peers = []
        if stage == 0:
            peers.append(dev(partner))
        elif stage == 1:
            for t in range(1, nx):
                peers.append(dev(cidx(z, ylo, lax.rem(x + t, nx))))
        elif stage == 2:
            both = dp * ny + ylo
            for t in range(1, ny * n_dp):
                other = lax.rem(both + t, ny * n_dp)
                peers.append(dev(cidx(z, lax.rem(other, ny), x), lax.div(other, ny)))
        elif stage == 3:
            for t in ((1, nz - 1, nz - 2) if nz > 4 else range(1, nz)):
                peers.append(dev(cidx(lax.rem(z + t, nz), ylo, x)))
        elif nz > 4:
            peers.append(dev(cidx(lax.rem(z + 4, nz), ylo, x)))
        return peers

    def remote(src, dst, send_sem, recv_sem, target):
        return pltpu.make_async_remote_copy(src, dst, send_sem, recv_sem, device_id=target, device_id_type=MESH)

    def count_copy(stage, t, target):
        return remote(acc.at[stage], cbuf.at[stage, t], c_s.at[stage, t], c_r.at[stage, t], target)

    def count_send(stage):
        for t, target in enumerate(count_peers(stage)):
            count_copy(stage, t, target).start()

    def count_take(stage):
        total = acc[stage]
        for t, target in enumerate(count_peers(stage)):
            cp = count_copy(stage, t, target)
            cp.wait_recv()
            cp.wait_send()
            total = total + cbuf[stage, t]
        acc[stage + 1] = total

    barrier = pltpu.get_barrier_semaphore()

    def greet(target):
        pl.semaphore_signal(barrier, inc=1, device_id=target, device_id_type=MESH)

    greet(dev(across))
    pl.when(has_back)(lambda: greet(dev(i - 2)))
    n_greet = 1
    for stage in range(4):
        for target in count_peers(stage):
            greet(target)
            n_greet += 1
    if nz > 4:
        greet(dev(cidx(lax.rem(z + 2, nz), ylo, x)))
        n_greet += 1

    ins = []
    for g in range(GROUPS):
        for h in range(2):
            for w, src in enumerate((k_hbm, v_hbm)):
                cp = pltpu.make_async_copy(src.at[h, :, pl.ds(g * 128, 128)], win.at[g, h, 0, w], kv_sem.at[g, h, w])
                cp.start()
                ins.append(cp)
    cq = pltpu.make_async_copy(q_hbm, q_ref, in_sem.at[0])
    cd = pltpu.make_async_copy(do_hbm, do_ref, in_sem.at[1])
    cq.start()
    cd.start()

    mask = mask_ref[...]
    acc[0] = jnp.pad(mask[0:1] + mask[1:2], ((0, 7), (0, 64)))

    @pl.when(i < 2)
    def _():
        zeros = jnp.zeros((GROUPS, 2, SPAN, HEAD), jnp.bfloat16)
        win[:, 0, 1] = zeros
        win[:, 0, 2] = zeros
        rx2[:, 1, 0] = zeros

    @pl.when(i < 4)
    def _():
        rx2[:, 1, 1] = jnp.zeros((GROUPS, 2, SPAN, HEAD), jnp.bfloat16)

    pl.semaphore_wait(barrier, n_greet + has_back.astype(jnp.int32))

    def up_copy(g, h, forward):
        if h == 0:
            half, target = jnp.where(inside, 0, 1), dev(across)
        else:
            half, target = 1, dev(i - 2)
        sems = (fw_s, fw_r) if forward else (up_s, up_r)
        slot = 1 if forward else 0
        return remote(win.at[g, h, slot], win.at[g, half, slot + 1], sems[0].at[g, h], sems[1].at[g, half], target)

    def up_send(g, forward):
        up_copy(g, 0, forward).start()
        pl.when(has_back)(lambda: up_copy(g, 1, forward).start())

    def up_arrived(g, h, forward):
        sems = (fw_s, fw_r) if forward else (up_s, up_r)
        slot = 2 if forward else 1
        remote(win.at[g, h, slot], win.at[g, h, slot], sems[0].at[g, h], sems[1].at[g, h], dev(partner)).wait_recv()

    def partner_copy(g, h):
        return remote(win.at[g, h, pl.ds(rs[h], 2)], win.at[g, h, pl.ds(3, 2)], pt_s.at[g, h], pt_r.at[g, h], dev(partner))

    def relay(g, forward):
        pl.when(has_back)(lambda: up_arrived(g, 0, forward))
        up_arrived(g, 1, forward)
        if not forward:
            up_send(g, True)
        else:
            for h in range(2):
                partner_copy(g, h).start()

    for g in range(GROUPS):
        for cp in ins[4 * g:4 * g + 4]:
            cp.wait()
        up_send(g, False)
    count_send(0)
    cq.wait()
    cd.wait()

    lane = lax.broadcasted_iota(jnp.int32, (1, 128), 1)
    tri = lax.broadcasted_iota(jnp.int32, (64, 128), 0) <= (lane & 63)

    def prepare(h):
        m = mask[h:h + 1].astype(jnp.float32)
        m2 = jnp.concatenate([m, m], axis=1)
        mt_ref[h] = jnp.broadcast_to(m2, (128, 128)).T.astype(jnp.bfloat16)
        rel = relative_positions()
        start_row = start_ref[h:h + 1]
        start2 = jnp.concatenate([start_row, start_row], axis=1) - spans[h] * SPAN
        bias_ref[h] = jnp.where(rel >= start2, 0.0, MASKED)
        base = seed_ref[0] * 1000003 + spans[h] * (SPAN * 9973)
        col0 = (spans[h] * SPAN + (lane & 63)) * 40503 + base + (lane >> 6) * 7919

        def fill(pair, carry):
            keep = keep_mask(relative_positions() * 9973 + (col0 + pair * (2 * 7919)))
            keep_ref[h, pair] = jnp.where(keep, 1.0, 0.0)
            for k in range(2):
                cols = pl.ds(pl.multiple_of(pair * 256 + k * 128, 128), 128)
                do_ref[h, :, cols] = do_ref[h, :, cols] * mt_ref[h, 0:64]
            return carry

        lax.fori_loop(0, HEADS // 2, fill, 0)

    prepare(0)
    count_take(0)
    count_send(1)
    relay(0, False)
    prepare(1)
    for g in range(1, GROUPS):
        relay(g, False)
    relay(0, True)
    count_take(1)
    count_send(2)

    s_refs, d_refs = (s0_ref, s1_ref), (d0_ref, d1_ref)
    pm_refs = ((pm00_ref, pm01_ref), (pm10_ref, pm11_ref))
    ds_refs = ((ds00_ref, ds01_ref), (ds10_ref, ds11_ref))

    def kv_here(g, h):
        partner_copy(g, h).wait_recv()

    def stack(ref, g, h, hh):
        return jnp.concatenate(
            [ref[h, :, pl.ds(pl.multiple_of(g * 1024 + (hh * 4 + j) * 128, 128), 128)] for j in range(4)], axis=0)

    def scores(g, h, hh, which=(0, 1)):
        if 0 in which:
            s_refs[hh][...] = nt(win[g, h, :, 0].reshape(320, 128), stack(q_ref, g, h, hh))
        if 1 in which:
            d_refs[hh][...] = nt(win[g, h, :, 1].reshape(320, 128), stack(do_ref, g, h, hh))

    def soft(g, h, hh, prs=(0, 1)):
        s_ref, d_ref = s_refs[hh], d_refs[hh]
        for pr in prs:
            cs = slice(pr * 128, pr * 128 + 128)
            s = jnp.concatenate([s_ref[64:128, cs], s_ref[192:320, cs], jnp.where(tri, s_ref[0:64, cs], s_ref[128:192, cs])], axis=0)
            s = s + bias_ref[h]
            top = jnp.max(s, axis=0, keepdims=True)
            e = jnp.exp2((s - top) * EXP2_SCALE)
            p = e * (1.0 / jnp.sum(e, axis=0, keepdims=True))
            pm = p * keep_ref[h, g * 4 + hh * 2 + pr]
            dpv = jnp.concatenate([d_ref[64:128, cs], d_ref[192:320, cs], jnp.where(tri, d_ref[0:64, cs], d_ref[128:192, cs])], axis=0)
            t = pm * dpv
            ds = t - p * jnp.sum(t, axis=0, keepdims=True)
            for ref, val in ((pm_refs[h][hh], pm), (ds_refs[h][hh], ds)):
                ref[g, 0:64, cs] = jnp.where(tri, val[192:], 0.0).astype(jnp.bfloat16)
                ref[g, 64:128, cs] = val[:64].astype(jnp.bfloat16)
                ref[g, 128:192, cs] = jnp.where(tri, 0.0, val[192:]).astype(jnp.bfloat16)
                ref[g, 192:320, cs] = val[64:192].astype(jnp.bfloat16)

    def products(g, h, hh):
        for w, (ref, other) in enumerate(((ds_refs[h][hh], q_ref), (pm_refs[h][hh], do_ref))):
            val = nn(ref[g], stack(other, g, h, hh))
            if hh == 0:
                sum_ref[w] = val
            else:
                val = val + sum_ref[w]
                own[g, h, w] = val[0:64]
                part[g, h, :, w] = val.reshape(5, SPAN, HEAD).astype(jnp.bfloat16)

    def outputs(g, h):
        kt = win[g, h, :, 0].reshape(320, 128).T
        vt = win[g, h, :, 1].reshape(320, 128).T
        for hh in range(2):
            oo = (nn(vt, pm_refs[h][hh][g]) * KEEP_SCALE).astype(jnp.bfloat16).T
            dq = nn(kt, ds_refs[h][hh][g]).astype(jnp.bfloat16).T
            for j in range(4):
                cols = pl.ds(pl.multiple_of(g * 1024 + (hh * 4 + j) * 128, 128), 128)
                o_ref[h, :, cols] = oo[j * 64:(j + 1) * 64]
                dqo_ref[h, :, cols] = dq[j * 64:(j + 1) * 64]

    def block(sc, so, pr):
        products(*pr)
        soft(*so)
        scores(*sc)

    def grad1_copy(g, h):
        return remote(part.at[g, h, pl.ds(3, 2)], rx1.at[g, h], g1_s.at[g, h], g1_r.at[g, h], dev(partner))

    def share(g, h):
        grad1_copy(g, h).start()

    def down_copy(g, h, e):
        if h == 0:
            half, target = 0, dev(i - 2 - 2 * e)
        else:
            half = jnp.where((inside, inside4)[e], 1, 0)
            target = dev((across, across4)[e])
        return remote(tot.at[g, h, e], rx2.at[g, half, e], g2_s.at[g, h, e], g2_r.at[g, half, e], target)

    def down_arrived(g, h, e):
        def take():
            remote(rx2.at[g, h, e], rx2.at[g, h, e], g2_s.at[g, h, e], g2_r.at[g, h, e], dev(partner)).wait_recv()

        if h == 0:
            take()
        else:
            pl.when((has_back, has_back4)[e])(take)

    def combine(g, h):
        r = rs[h]
        grad1_copy(g, h).wait_recv()
        tot[g, h, 1] = part[g, h, 2] + rx1[g, h, 1] * r.astype(jnp.bfloat16)
        tot[g, h, 0] = part[g, h, 1] + rx1[g, h, 1 - r]
        for e in (1, 0):
            if h == 0:
                pl.when((has_back, has_back4)[e])(lambda e=e: down_copy(g, h, e).start())
            else:
                down_copy(g, h, e).start()

    kv_here(0, 0)
    scores(0, 0, 0)
    pm11_ref[0] = jnp.zeros((320, 256), jnp.bfloat16)
    ds11_ref[0] = jnp.zeros((320, 256), jnp.bfloat16)

    def step(g, carry):
        before = jnp.maximum(g - 1, 0)
        after = jnp.minimum(g + 1, GROUPS - 1)
        block((g, 0, 1), (g, 0, 0), (before, 1, 1))

        @pl.when(g > 0)
        def _():
            share(g - 1, 1)
            combine(g - 1, 0)

        pl.when(g < GROUPS - 1)(lambda: relay(g + 1, True))
        kv_here(g, 1)
        block((g, 1, 0), (g, 0, 1), (g, 0, 0))
        block((g, 1, 1), (g, 1, 0), (g, 0, 1))
        share(g, 0)
        pl.when(g > 0)(lambda: combine(g - 1, 1))

        @pl.when(g == 1)
        def _():
            count_take(2)
            count_send(3)

        @pl.when(g == 3)
        def _():
            count_take(3)
            count_send(4)

        pl.when(g < GROUPS - 1)(lambda: kv_here(g + 1, 0))
        block((after, 0, 0), (g, 1, 1), (g, 1, 0))
        return carry

    lax.fori_loop(0, GROUPS, step, 0)
    products(GROUPS - 1, 1, 1)
    share(GROUPS - 1, 1)
    combine(GROUPS - 1, 0)
    def finish(g, carry):
        for h in range(2):
            outputs(g, h)
        return carry

    finish(0, 0)
    combine(GROUPS - 1, 1)
    lax.fori_loop(1, GROUPS, finish, 0)

    def drain(g, carry):
        for h in range(2):
            partner_copy(g, h).wait_send()
            grad1_copy(g, h).wait_send()
            down_copy(g, 1, h).wait_send()
            pl.when((has_back, has_back4)[h])(lambda h=h: down_copy(g, 0, h).wait_send())
        for flag in (False, True):
            up_copy(g, 0, flag).wait_send()
            pl.when(has_back)(lambda flag=flag: up_copy(g, 1, flag).wait_send())
        return carry

    lax.fori_loop(0, GROUPS, drain, 0)

    for g in range(GROUPS):
        for h in range(2):
            for e in range(2):
                down_arrived(g, h, e)
    count_take(4)
    total = jnp.sum(acc[5].astype(jnp.float32))
    slots = float(2 * 2 * n * SPAN)
    factor = jnp.full((1, 128), slots * KEEP_SCALE, jnp.float32) / jnp.full((1, 128), total, jnp.float32)

    def final(g, carry):
        for h in range(2):
            val = own[g, h] + (1 - rs[h]).astype(jnp.float32) * rx1[g, h, 0].astype(jnp.float32)
            val = val + rx2[g, h, 0].astype(jnp.float32) + rx2[g, h, 1].astype(jnp.float32)
            cols = pl.ds(pl.multiple_of(g * 128, 128), 128)
            dkv_ref[0, h, :, cols] = val[0] * (factor * INV)
            dkv_ref[1, h, :, cols] = val[1] * factor
            for j in range(8):
                cols = pl.ds(pl.multiple_of(g * 1024 + j * 128, 128), 128)
                dqo_ref[h, :, cols] = (dqo_ref[h, :, cols].astype(jnp.float32) * (factor * INV)).astype(jnp.bfloat16)
        return carry

    lax.fori_loop(0, GROUPS, final, 0)


def store_kernel(o_ref, dq_ref, dkv_ref, o_hbm, dq_hbm, dk_hbm, dv_hbm, sems):
    copies = [
        pltpu.make_async_copy(o_ref, o_hbm, sems.at[0]),
        pltpu.make_async_copy(dq_ref, dq_hbm, sems.at[1]),
        pltpu.make_async_copy(dkv_ref.at[0], dk_hbm, sems.at[2]),
        pltpu.make_async_copy(dkv_ref.at[1], dv_hbm, sems.at[3]),
    ]
    for cp in copies:
        cp.start()
    for cp in copies:
        cp.wait()


def grid_of(n):
    nc, nx = 2, 4
    ny = 2 if n // (nc * nx) > 1 else 1
    return (n // (nc * nx * ny), ny, nx, nc)


def body(queries, keys, values, cotangent, doc_start, loss_mask, seeds):
    n = lax.axis_size("ctx")
    dims = grid_of(n)
    peers = max(1, dims[2] - 1, dims[1] * lax.axis_size("dp") - 1, dims[0] - 1)
    wide = (2, SPAN, HEADS * HEAD)
    narrow = (2, SPAN, GROUPS * HEAD)
    bf16, f32, i32 = jnp.bfloat16, jnp.float32, jnp.int32
    hbm = pl.BlockSpec(memory_space=pl.ANY)
    vmem = pl.BlockSpec(memory_space=pltpu.VMEM)
    dma = pltpu.SemaphoreType.DMA
    pair = (2, SPAN, HEAD)
    held = pl.pallas_call(
        functools.partial(kernel, n, dims),
        out_shape=[pltpu.VMEM(wide, bf16), pltpu.VMEM(wide, bf16), pltpu.VMEM((2,) + narrow, f32)],
        in_specs=[hbm] * 4 + [vmem, vmem, pl.BlockSpec(memory_space=pltpu.SMEM)],
        out_specs=[vmem] * 3,
        scratch_shapes=[
            pltpu.VMEM(wide, bf16),
            pltpu.VMEM(wide, bf16),
            pltpu.VMEM((GROUPS, 2, 5) + pair, bf16),
            pltpu.VMEM((GROUPS, 2, 5) + pair, bf16),
            pltpu.VMEM((GROUPS, 2) + pair, f32),
            pltpu.VMEM((GROUPS, 2, 2) + pair, bf16),
            pltpu.VMEM((GROUPS, 2, 2) + pair, bf16),
            pltpu.VMEM((GROUPS, 2, 2) + pair, bf16),
            pltpu.VMEM((2, HEADS // 2, 256, 128), f32),
            pltpu.VMEM((2, 256, 128), f32),
            pltpu.VMEM((2, 128, 128), bf16),
        ] + [pltpu.VMEM((320, 256), f32)] * 4 + [pltpu.VMEM((GROUPS, 320, 256), bf16)] * 8 + [
            pltpu.VMEM((2, 320, 128), f32),
            pltpu.VMEM((6, 8, 128), i32),
            pltpu.VMEM((5, peers, 8, 128), i32),
            dma((2,)),
            dma((GROUPS, 2, 2)),
        ] + [dma((GROUPS, 2))] * 8 + [dma((GROUPS, 2, 2))] * 2 + [dma((5, peers))] * 2,
        compiler_params=pltpu.CompilerParams(collective_id=0, has_side_effects=True),
        name="attention",
    )(
        queries.reshape(wide),
        cotangent.reshape(wide),
        keys.reshape(narrow),
        values.reshape(narrow),
        doc_start.reshape(2, SPAN),
        loss_mask.reshape(2, SPAN),
        seeds,
    )
    outs = pl.pallas_call(
        store_kernel,
        out_shape=[
            jax.ShapeDtypeStruct(wide, bf16),
            jax.ShapeDtypeStruct(wide, bf16),
            jax.ShapeDtypeStruct(narrow, f32),
            jax.ShapeDtypeStruct(narrow, f32),
        ],
        in_specs=[vmem] * 3,
        out_specs=[hbm] * 4,
        scratch_shapes=[dma((4,))],
        name="store",
    )(*[pltpu.with_memory_space_constraint(x, pltpu.VMEM) for x in held])
    return (
        outs[0].reshape(queries.shape),
        outs[1].reshape(queries.shape),
        outs[2].reshape(keys.shape),
        outs[3].reshape(values.shape),
    )


def solution(mesh):
    wide = P("dp", None, "ctx", None, None)
    flat = P("dp", None, "ctx", None)
    return jax.shard_map(
        body,
        mesh=mesh,
        in_specs=(wide, wide, wide, wide, flat, flat, P("dp")),
        out_specs=(wide, wide, wide, wide),
        check_vma=False,
    )
```

time: 41.4 us -> 37.3 us (0.901)
  the two profiles are of different devices: /device:TPU:9 before, /device:TPU:1 now
where the time goes in v2:
time: 37.3 us; the launch traced here: 37.1 us
  Pallas kernels  35.9 us (96%)
  between operations  1.29 us (3%)
    pallas_call x1, Pallas kernels, body(): pl.pallas_call(functools.partial(kernel, n, dims), out_shape=[pltpu.VMEM(...  34.3 us
    pallas_call x1, Pallas kernels, body(): pl.pallas_call(store_kernel, out_shape=[jax.ShapeDtypeStruct(wide, bf16),...  1.52 us

profile of v2, /device:TPU:1, one launch (start us, length us, event | category | flops | bytes accessed | tf_op | source)
XLA Modules:
  0.0 37.1 jit_solution(3055850659056835257)
XLA Ops:
  1.3 34.3 %attention.1 = (bf16[2,64,4096]{2,1,0:T(8,128)(2,1)S(1)}, bf16[2,64,4096]{2,1,0:T(8,128)(2,1)S(1)}, f32[2,2,64,512]{3,2,1,0:T(8,128)S(1)}) custom-call(bf16[2,64,4096]{2,1,0:T(8,128)(2,1)} %bitcast.18, bf16[2,64,4096]{2,1,0:T(8,128)(2,1)} %bitcast.19, bf16[2,64,512]{2,1,0:T(8,128)(2,1)} %bitcast.20, bf16[2,64,512]{2,1,0:T(8,128)(2,1)} %bitcast.21, ...), custom_call_target="tpu_custom_call" | custom-call | tf_op jit(solution)/shard_map/attention/pallas_call | solution.py:448
  35.6 1.5 %store.1 = (bf16[2,64,4096]{2,1,0:T(8,128)(2,1)}, bf16[2,64,4096]{2,1,0:T(8,128)(2,1)}, f32[2,64,512]{2,1,0:T(8,128)}, f32[2,64,512]{2,1,0:T(8,128)}) custom-call(bf16[2,64,4096]{2,1,0:T(8,128)(2,1)S(1)} %get-tuple-element.11.o_ref, bf16[2,64,4096]{2,1,0:T(8,128)(2,1)S(1)} %get-tuple-element.12.dq_ref, f32[2,2,64,512]{3,2,1,0:T(8,128)S(1)} %get-tuple-element.13.dkv_ref), custom_call_target="tpu_custom_call" | custom-call | tf_op jit(solution)/shard_map/store/pallas_call | solution.py:483

commit v3 on v2

--- a/solution.py
+++ b/solution.py
@@ -46,9 +46,9 @@
     return inner - 64 * behind
 
 
-def kernel(n, dims, q_hbm, do_hbm, k_hbm, v_hbm, start_ref, mask_ref, seed_ref,
+def kernel(n, dims, q_hbm, do_hbm, k_hbm, v_hbm, start_hbm, mask_hbm, seed_hbm,
            o_ref, dqo_ref, dkv_ref,
-           q_ref, do_ref,
+           q_ref, do_ref, start_ref, mask_ref, seed_ref,
            win, part, own, rx1, tot, rx2, keep_ref, bias_ref, mt_ref,
            s0_ref, s1_ref, d0_ref, d1_ref, pm00_ref, pm01_ref, pm10_ref, pm11_ref, ds00_ref, ds01_ref, ds10_ref, ds11_ref, sum_ref,
            acc, cbuf,
@@ -141,11 +141,15 @@
                 ins.append(cp)
     cq = pltpu.make_async_copy(q_hbm, q_ref, in_sem.at[0])
     cd = pltpu.make_async_copy(do_hbm, do_ref, in_sem.at[1])
+    small = [
+        pltpu.make_async_copy(src, dst, in_sem.at[2 + k])
+        for k, (src, dst) in enumerate(((start_hbm, start_ref), (mask_hbm, mask_ref), (seed_hbm, seed_ref)))
+    ]
+    for cp in small:
+        cp.start()
     cq.start()
     cd.start()
 
-    mask = mask_ref[...]
-    acc[0] = jnp.pad(mask[0:1] + mask[1:2], ((0, 7), (0, 64)))
 
     @pl.when(i < 2)
     def _():
@@ -194,6 +198,10 @@
         for cp in ins[4 * g:4 * g + 4]:
             cp.wait()
         up_send(g, False)
+    for cp in small:
+        cp.wait()
+    mask = mask_ref[...]
+    acc[0] = jnp.pad(mask[0:1] + mask[1:2], ((0, 7), (0, 64)))
     count_send(0)
     cq.wait()
     cd.wait()
@@ -391,14 +399,24 @@
 
     lax.fori_loop(0, GROUPS, drain, 0)
 
-    for g in range(GROUPS):
+    def arrived(g):
         for h in range(2):
             for e in range(2):
                 down_arrived(g, h, e)
+
+    for g in range(GROUPS - 1):
+        arrived(g)
     count_take(4)
     total = jnp.sum(acc[5].astype(jnp.float32))
     slots = float(2 * 2 * n * SPAN)
     factor = jnp.full((1, 128), slots * KEEP_SCALE, jnp.float32) / jnp.full((1, 128), total, jnp.float32)
+
+    def rescale(g, carry):
+        for h in range(2):
+            for j in range(8):
+                cols = pl.ds(pl.multiple_of(g * 1024 + j * 128, 128), 128)
+                dqo_ref[h, :, cols] = (dqo_ref[h, :, cols].astype(jnp.float32) * (factor * INV)).astype(jnp.bfloat16)
+        return carry
 
     def final(g, carry):
         for h in range(2):
@@ -407,12 +425,12 @@
             cols = pl.ds(pl.multiple_of(g * 128, 128), 128)
             dkv_ref[0, h, :, cols] = val[0] * (factor * INV)
             dkv_ref[1, h, :, cols] = val[1] * factor
-            for j in range(8):
-                cols = pl.ds(pl.multiple_of(g * 1024 + j * 128, 128), 128)
-                dqo_ref[h, :, cols] = (dqo_ref[h, :, cols].astype(jnp.float32) * (factor * INV)).astype(jnp.bfloat16)
         return carry
 
-    lax.fori_loop(0, GROUPS, final, 0)
+    lax.fori_loop(0, GROUPS, rescale, 0)
+    lax.fori_loop(0, GROUPS - 1, final, 0)
+    arrived(GROUPS - 1)
+    final(GROUPS - 1, 0)
 
 
 def store_kernel(o_ref, dq_ref, dkv_ref, o_hbm, dq_hbm, dk_hbm, dv_hbm, sems):
@@ -448,11 +466,14 @@
     held = pl.pallas_call(
         functools.partial(kernel, n, dims),
         out_shape=[pltpu.VMEM(wide, bf16), pltpu.VMEM(wide, bf16), pltpu.VMEM((2,) + narrow, f32)],
-        in_specs=[hbm] * 4 + [vmem, vmem, pl.BlockSpec(memory_space=pltpu.SMEM)],
+        in_specs=[hbm] * 7,
         out_specs=[vmem] * 3,
         scratch_shapes=[
             pltpu.VMEM(wide, bf16),
             pltpu.VMEM(wide, bf16),
+            pltpu.VMEM((2, SPAN), i32),
+            pltpu.VMEM((2, SPAN), i32),
+            pltpu.SMEM((1,), i32),
             pltpu.VMEM((GROUPS, 2, 5) + pair, bf16),
             pltpu.VMEM((GROUPS, 2, 5) + pair, bf16),
             pltpu.VMEM((GROUPS, 2) + pair, f32),
@@ -466,7 +487,7 @@
             pltpu.VMEM((2, 320, 128), f32),
             pltpu.VMEM((6, 8, 128), i32),
             pltpu.VMEM((5, peers, 8, 128), i32),
-            dma((2,)),
+            dma((5,)),
             dma((GROUPS, 2, 2)),
         ] + [dma((GROUPS, 2))] * 8 + [dma((GROUPS, 2, 2))] * 2 + [dma((5, peers))] * 2,
         compiler_params=pltpu.CompilerParams(collective_id=0, has_side_effects=True),

time: 37.3 us -> 36.6 us (0.981)
  Pallas kernels: 35.9 us -> 35.2 us
    pallas_call x1, Pallas kernels: 34.3 us -> 33.7 us  [body(): pl.pallas_call(functools.partial(kernel, n, dims), out_shape=[pltpu.VMEM(...]
where the time goes in v3:
time: 36.6 us; the launch traced here: 36.5 us
  Pallas kernels  35.2 us (96%)
  between operations  1.29 us (4%)
    pallas_call x1, Pallas kernels, body(): pl.pallas_call(functools.partial(kernel, n, dims), out_shape=[pltpu.VMEM(...  33.7 us
    pallas_call x1, Pallas kernels, body(): pl.pallas_call(store_kernel, out_shape=[jax.ShapeDtypeStruct(wide, bf16),...  1.52 us

profile of v3, /device:TPU:1, one launch (start us, length us, event | category | flops | bytes accessed | tf_op | source)
XLA Modules:
  0.0 36.5 jit_solution(7539398853575065921)
XLA Ops:
  1.3 33.7 %attention.1 = (bf16[2,64,4096]{2,1,0:T(8,128)(2,1)S(1)}, bf16[2,64,4096]{2,1,0:T(8,128)(2,1)S(1)}, f32[2,2,64,512]{3,2,1,0:T(8,128)S(1)}) custom-call(bf16[2,64,4096]{2,1,0:T(8,128)(2,1)} %bitcast.18, bf16[2,64,4096]{2,1,0:T(8,128)(2,1)} %bitcast.19, bf16[2,64,512]{2,1,0:T(8,128)(2,1)} %bitcast.20, bf16[2,64,512]{2,1,0:T(8,128)(2,1)} %bitcast.21, ...), custom_call_target="tpu_custom_call" | custom-call | tf_op jit(solution)/shard_map/attention/pallas_call | solution.py:466
  35.0 1.5 %store.1 = (bf16[2,64,4096]{2,1,0:T(8,128)(2,1)}, bf16[2,64,4096]{2,1,0:T(8,128)(2,1)}, f32[2,64,512]{2,1,0:T(8,128)}, f32[2,64,512]{2,1,0:T(8,128)}) custom-call(bf16[2,64,4096]{2,1,0:T(8,128)(2,1)S(1)} %get-tuple-element.11.o_ref, bf16[2,64,4096]{2,1,0:T(8,128)(2,1)S(1)} %get-tuple-element.12.dq_ref, f32[2,2,64,512]{3,2,1,0:T(8,128)S(1)} %get-tuple-element.13.dkv_ref), custom_call_target="tpu_custom_call" | custom-call | tf_op jit(solution)/shard_map/store/pallas_call | solution.py:504

commit v4 on v3

--- a/solution.py
+++ b/solution.py
@@ -185,14 +185,18 @@
     def partner_copy(g, h):
         return remote(win.at[g, h, pl.ds(rs[h], 2)], win.at[g, h, pl.ds(3, 2)], pt_s.at[g, h], pt_r.at[g, h], dev(partner))
 
-    def relay(g, forward):
-        pl.when(has_back)(lambda: up_arrived(g, 0, forward))
-        up_arrived(g, 1, forward)
-        if not forward:
-            up_send(g, True)
-        else:
-            for h in range(2):
+    def relay(g, forward, halves=(0, 1)):
+        for h in halves:
+            if h == 0:
+                pl.when(has_back)(lambda: up_arrived(g, 0, forward))
+            else:
+                up_arrived(g, 1, forward)
+            if forward:
                 partner_copy(g, h).start()
+            elif h == 0:
+                up_copy(g, 0, True).start()
+            else:
+                pl.when(has_back)(lambda: up_copy(g, 1, True).start())
 
     for g in range(GROUPS):
         for cp in ins[4 * g:4 * g + 4]:
@@ -345,19 +349,18 @@
     def step(g, carry):
         before = jnp.maximum(g - 1, 0)
         after = jnp.minimum(g + 1, GROUPS - 1)
+        pl.when(g < GROUPS - 1)(lambda: relay(g + 1, True))
         block((g, 0, 1), (g, 0, 0), (before, 1, 1))
 
         @pl.when(g > 0)
         def _():
             share(g - 1, 1)
-            combine(g - 1, 0)
-
-        pl.when(g < GROUPS - 1)(lambda: relay(g + 1, True))
+
         kv_here(g, 1)
         block((g, 1, 0), (g, 0, 1), (g, 0, 0))
         block((g, 1, 1), (g, 1, 0), (g, 0, 1))
         share(g, 0)
-        pl.when(g > 0)(lambda: combine(g - 1, 1))
+        pl.when(g > 0)(lambda: combine(g - 1, 0))
 
         @pl.when(g == 1)
         def _():
@@ -371,6 +374,7 @@
 
         pl.when(g < GROUPS - 1)(lambda: kv_here(g + 1, 0))
         block((after, 0, 0), (g, 1, 1), (g, 1, 0))
+        pl.when(g > 0)(lambda: combine(g - 1, 1))
         return carry
 
     lax.fori_loop(0, GROUPS, step, 0)

time: 36.6 us -> 35.7 us (0.975)
  the two profiles are of different devices: /device:TPU:1 before, /device:TPU:9 now
where the time goes in v4:
time: 35.7 us; the launch traced here: 35.4 us
  Pallas kernels  34.1 us (96%)
  between operations  1.29 us (4%)
    pallas_call x1, Pallas kernels, body(): pl.pallas_call(functools.partial(kernel, n, dims), out_shape=[pltpu.VMEM(...  32.6 us
    pallas_call x1, Pallas kernels, body(): pl.pallas_call(store_kernel, out_shape=[jax.ShapeDtypeStruct(wide, bf16),...  1.52 us

profile of v4, /device:TPU:9, one launch (start us, length us, event | category | flops | bytes accessed | tf_op | source)
XLA Modules:
  0.0 35.4 jit_solution(14924375291540019125)
XLA Ops:
  1.3 32.6 %attention.1 = (bf16[2,64,4096]{2,1,0:T(8,128)(2,1)S(1)}, bf16[2,64,4096]{2,1,0:T(8,128)(2,1)S(1)}, f32[2,2,64,512]{3,2,1,0:T(8,128)S(1)}) custom-call(bf16[2,64,4096]{2,1,0:T(8,128)(2,1)} %bitcast.18, bf16[2,64,4096]{2,1,0:T(8,128)(2,1)} %bitcast.19, bf16[2,64,512]{2,1,0:T(8,128)(2,1)} %bitcast.20, bf16[2,64,512]{2,1,0:T(8,128)(2,1)} %bitcast.21, ...), custom_call_target="tpu_custom_call" | custom-call | tf_op jit(solution)/shard_map/attention/pallas_call | solution.py:470
  33.9 1.5 %store.1 = (bf16[2,64,4096]{2,1,0:T(8,128)(2,1)}, bf16[2,64,4096]{2,1,0:T(8,128)(2,1)}, f32[2,64,512]{2,1,0:T(8,128)}, f32[2,64,512]{2,1,0:T(8,128)}) custom-call(bf16[2,64,4096]{2,1,0:T(8,128)(2,1)S(1)} %get-tuple-element.11.o_ref, bf16[2,64,4096]{2,1,0:T(8,128)(2,1)S(1)} %get-tuple-element.12.dq_ref, f32[2,2,64,512]{3,2,1,0:T(8,128)S(1)} %get-tuple-element.13.dkv_ref), custom_call_target="tpu_custom_call" | custom-call | tf_op jit(solution)/shard_map/store/pallas_call | solution.py:508

commit v5 on v4

--- a/solution.py
+++ b/solution.py
@@ -238,8 +238,9 @@
     count_take(0)
     count_send(1)
     relay(0, False)
+    relay(1, False)
     prepare(1)
-    for g in range(1, GROUPS):
+    for g in range(2, GROUPS):
         relay(g, False)
     relay(0, True)
     count_take(1)

time: 35.7 us -> 35.7 us (level)
  no operation moved by 1% of the time
where the time goes in v5:
time: 35.7 us; the launch traced here: 35.4 us
  Pallas kernels  34.1 us (96%)
  between operations  1.29 us (4%)
    pallas_call x1, Pallas kernels, body(): pl.pallas_call(functools.partial(kernel, n, dims), out_shape=[pltpu.VMEM(...  32.6 us
    pallas_call x1, Pallas kernels, body(): pl.pallas_call(store_kernel, out_shape=[jax.ShapeDtypeStruct(wide, bf16),...  1.52 us

profile of v5, /device:TPU:9, one launch (start us, length us, event | category | flops | bytes accessed | tf_op | source)
XLA Modules:
  0.0 35.4 jit_solution(7541454894199202998)
XLA Ops:
  1.3 32.6 %attention.1 = (bf16[2,64,4096]{2,1,0:T(8,128)(2,1)S(1)}, bf16[2,64,4096]{2,1,0:T(8,128)(2,1)S(1)}, f32[2,2,64,512]{3,2,1,0:T(8,128)S(1)}) custom-call(bf16[2,64,4096]{2,1,0:T(8,128)(2,1)} %bitcast.18, bf16[2,64,4096]{2,1,0:T(8,128)(2,1)} %bitcast.19, bf16[2,64,512]{2,1,0:T(8,128)(2,1)} %bitcast.20, bf16[2,64,512]{2,1,0:T(8,128)(2,1)} %bitcast.21, ...), custom_call_target="tpu_custom_call" | custom-call | tf_op jit(solution)/shard_map/attention/pallas_call | solution.py:471
  33.9 1.5 %store.1 = (bf16[2,64,4096]{2,1,0:T(8,128)(2,1)}, bf16[2,64,4096]{2,1,0:T(8,128)(2,1)}, f32[2,64,512]{2,1,0:T(8,128)}, f32[2,64,512]{2,1,0:T(8,128)}) custom-call(bf16[2,64,4096]{2,1,0:T(8,128)(2,1)S(1)} %get-tuple-element.11.o_ref, bf16[2,64,4096]{2,1,0:T(8,128)(2,1)S(1)} %get-tuple-element.12.dq_ref, f32[2,2,64,512]{3,2,1,0:T(8,128)S(1)} %get-tuple-element.13.dkv_ref), custom_call_target="tpu_custom_call" | custom-call | tf_op jit(solution)/shard_map/store/pallas_call | solution.py:509
